TPU v7x, 32 devices: a whole 2x2x4 slice. The times are simulated.
32 devices in a mesh: expert: 16 (over z, y, x), tok: 2 (over core).
Axes of the slice: x: 2, y: 2, z: 4, core: 2. Of those that a mesh axis runs over, the one named last changes fastest.
Arguments:
- tokens: bfloat16 [2048, 3584], P(('expert', 'tok')), may hold values from -6 to 6
- routes: int32 [2048, 8], P(('expert', 'tok')), may hold values from 0 to 15, all different within a row; in each aligned block of 64 rows (0 to 63, 64 to 127, ...) at most 36 rows name the same one
- gates: float32 [2048, 8], P(('expert', 'tok')), may hold values from 0.05 to 1
- upstream: bfloat16 [2048, 3584], P(('expert', 'tok')), may hold values from -6 to 6
- w_up: bfloat16 [16, 3584, 1024], P('expert', None, 'tok'), may hold values from -0.09375 to 0.09375
- w_down: bfloat16 [16, 1024, 3584], P('expert', 'tok'), may hold values from -0.1875 to 0.1875
Outputs:
- mixed: bfloat16 [2048, 3584], P(('expert', 'tok'))
- d_tokens: bfloat16 [2048, 3584], P(('expert', 'tok'))
- d_gates: float32 [2048, 8], P(('expert', 'tok'))
- grad_up: bfloat16 [16, 3584, 1024], P('expert', None, 'tok')
- grad_down: bfloat16 [16, 1024, 3584], P('expert', 'tok')
Inputs may be any that keep to these rules, and one draw needn't show every extreme that they name: `routes`: each token names 8 different experts. At most 36 of the 64 tokens of one device name the same expert, and in every draw the tokens of some device name some expert exactly 36 times.
All inputs are finite; a program needn't handle non-finite values.
Results may differ from a plain program's by a relative error of at most 0.0065.
Values may be sent and summed in bfloat16 or wider, within the bound.
A program may use at most 192 MiB of HBM per device.

v0:
```python
import jax
import jax.numpy as jnp
from jax import lax
from jax.sharding import PartitionSpec as P

GELU_C = 0.7978845608028654
GELU_A = 0.044715


def gelu_value(hidden):
    inner_arg = GELU_C * (hidden + GELU_A * hidden * hidden * hidden)
    return 0.5 * hidden * (1.0 + jnp.tanh(inner_arg))


def gelu_slope(hidden):
    tangent = jnp.tanh(GELU_C * (hidden + GELU_A * hidden * hidden * hidden))
    return 0.5 * (1.0 + tangent) + 0.5 * hidden * (1.0 - tangent * tangent) * GELU_C * (
        1.0 + 3.0 * GELU_A * hidden * hidden
    )


def expert_rows(rows_x, rows_grad, up_local, down_local):
    hidden = jnp.dot(rows_x, up_local, preferred_element_type=jnp.float32)
    active = gelu_value(hidden).astype(jnp.bfloat16)
    out_part = jnp.dot(active, down_local, preferred_element_type=jnp.float32)
    d_active = lax.dot_general(
        rows_grad, down_local, (((1,), (1,)), ((), ())), preferred_element_type=jnp.float32
    )
    d_hidden = (d_active * gelu_slope(hidden)).astype(jnp.bfloat16)
    dx_part = lax.dot_general(
        d_hidden, up_local, (((1,), (1,)), ((), ())), preferred_element_type=jnp.float32
    )
    grad_down = lax.dot_general(
        active, rows_grad, (((0,), (0,)), ((), ())), preferred_element_type=jnp.float32
    )
    grad_up = lax.dot_general(
        rows_x, d_hidden, (((0,), (0,)), ((), ())), preferred_element_type=jnp.float32
    )
    return (out_part, dx_part, grad_up, grad_down)


def routed_shards(tokens, routes, gates, upstream, w_up, w_down):
    tok_rows, feature_width = tokens.shape
    top_count = routes.shape[1]
    owners = lax.axis_size("expert")
    pair_count = lax.axis_size("tok")
    capacity = tok_rows * top_count // owners + max(1, tok_rows * top_count // (8 * owners))
    assigned = routes.reshape(-1)
    labels = jnp.arange(owners, dtype=jnp.int32)
    onehot = (assigned[:, None] == labels[None, :]).astype(jnp.int32)
    earlier = jnp.cumsum(onehot, axis=0) - onehot
    slot_rank = jnp.sum(earlier * onehot, axis=1)
    slot_of = assigned * capacity + slot_rank
    slot_ids = jnp.arange(owners * capacity, dtype=jnp.int32)
    matches = (slot_of[None, :] == slot_ids[:, None]).astype(jnp.int32)
    filled = jnp.sum(matches, axis=1) > 0
    source = jnp.sum(matches * jnp.arange(assigned.shape[0], dtype=jnp.int32)[None, :], axis=1)
    token_ids = source // top_count
    send_x = jnp.where(filled[:, None], tokens[token_ids], jnp.zeros((), jnp.bfloat16))
    gate_rows = jnp.where(filled, gates.reshape(-1)[source], jnp.zeros((), jnp.float32))
    send_grad = (gate_rows[:, None] * upstream[token_ids].astype(jnp.float32)).astype(jnp.bfloat16)
    send_x = send_x.reshape(owners, capacity, feature_width)
    send_grad = send_grad.reshape(owners, capacity, feature_width)
    recv_x, recv_grad = (
        lax.all_to_all(send_x, "expert", split_axis=0, concat_axis=0, tiled=True),
        lax.all_to_all(send_grad, "expert", split_axis=0, concat_axis=0, tiled=True),
    )
    both_x, both_grad = (
        lax.all_gather(recv_x[None], "tok", axis=0, tiled=True),
        lax.all_gather(recv_grad[None], "tok", axis=0, tiled=True),
    )
    rows_x = both_x.reshape(-1, feature_width)
    rows_grad = both_grad.reshape(-1, feature_width)
    out_part, dx_part, grad_up, grad_down = expert_rows(rows_x, rows_grad, w_up[0], w_down[0])
    shaped_out = out_part.reshape(pair_count, owners, capacity, feature_width)
    shaped_dx = dx_part.reshape(pair_count, owners, capacity, feature_width)
    summed_out, summed_dx = (
        lax.psum_scatter(shaped_out, "tok", scatter_dimension=0, tiled=True),
        lax.psum_scatter(shaped_dx, "tok", scatter_dimension=0, tiled=True),
    )
    home_out, home_dx = (
        lax.all_to_all(
            summed_out[0].astype(jnp.bfloat16), "expert", split_axis=0, concat_axis=0, tiled=True
        ),
        lax.all_to_all(
            summed_dx[0].astype(jnp.bfloat16), "expert", split_axis=0, concat_axis=0, tiled=True
        ),
    )
    out_pairs = (
        home_out.reshape(owners * capacity, feature_width)[slot_of]
        .reshape(tok_rows, top_count, feature_width)
        .astype(jnp.float32)
    )
    dx_pairs = (
        home_dx.reshape(owners * capacity, feature_width)[slot_of]
        .reshape(tok_rows, top_count, feature_width)
        .astype(jnp.float32)
    )
    mixed_out = jnp.sum(gates[:, :, None] * out_pairs, axis=1).astype(jnp.bfloat16)
    d_gates = jnp.sum(upstream.astype(jnp.float32)[:, None, :] * out_pairs, axis=2)
    d_tokens = jnp.sum(dx_pairs, axis=1).astype(jnp.bfloat16)
    return (
        mixed_out,
        d_tokens,
        d_gates,
        grad_up.astype(jnp.bfloat16)[None],
        grad_down.astype(jnp.bfloat16)[None],
    )


def dense_shards(tokens, routes, gates, upstream, w_up, w_down):
    tok_rows, width = tokens.shape
    owners = lax.axis_size("expert")
    half = w_up.shape[2]
    swap = ((0, 1), (1, 0))
    up_local, down_local = (w_up[0], w_down[0])
    up_full = jnp.concatenate([up_local, lax.ppermute(up_local, "tok", swap)], axis=1)
    down_full = jnp.concatenate([down_local, lax.ppermute(down_local, "tok", swap)], axis=0)
    named = routes[:, :, None] == jnp.arange(owners, dtype=jnp.int32)
    gate_of = jnp.sum(jnp.where(named, gates[:, :, None], 0.0), axis=1)
    gate = lax.all_to_all(gate_of.T, "expert", split_axis=0, concat_axis=0, tiled=True)
    gate = gate.reshape(-1)[:, None]
    all_x = lax.all_gather(tokens, "expert", axis=0, tiled=True)
    all_u = lax.all_gather(upstream, "expert", axis=0, tiled=True)
    hidden = jnp.dot(all_x, up_full, preferred_element_type=jnp.float32)
    gated = (gate * gelu_value(hidden)).astype(jnp.bfloat16)
    mixed_part = jnp.dot(gated, down_full, preferred_element_type=jnp.float32)
    mixed = lax.psum_scatter(
        mixed_part.astype(jnp.bfloat16), "expert", scatter_dimension=0, tiled=True
    )
    back = lax.dot_general(
        all_u, down_full, (((1,), (1,)), ((), ())), preferred_element_type=jnp.float32
    )
    inner = jnp.sum(gelu_value(hidden) * back, axis=1)
    d_hidden = (gate * back * gelu_slope(hidden)).astype(jnp.bfloat16)
    dx_part = lax.dot_general(
        d_hidden, up_full, (((1,), (1,)), ((), ())), preferred_element_type=jnp.float32
    )
    d_tokens = lax.psum_scatter(
        dx_part.astype(jnp.bfloat16), "expert", scatter_dimension=0, tiled=True
    )
    home = lax.all_to_all(
        inner.reshape(owners, tok_rows), "expert", split_axis=0, concat_axis=0, tiled=True
    )
    d_gates = jnp.sum(jnp.where(named, home.T[:, None, :], 0.0), axis=2)

    def outer(rows, columns):
        return lax.dot_general(
            rows, columns, (((0,), (0,)), ((), ())), preferred_element_type=jnp.float32
        )

    down_far = outer(gated[:, half:], all_u).astype(jnp.bfloat16)
    up_far = outer(all_x, d_hidden[:, half:]).astype(jnp.bfloat16)
    down_near = outer(gated[:, :half], all_u)
    up_near = outer(all_x, d_hidden[:, :half])
    grad_down = down_near + lax.ppermute(down_far, "tok", swap).astype(jnp.float32)
    grad_up = up_near + lax.ppermute(up_far, "tok", swap).astype(jnp.float32)
    return (
        mixed,
        d_tokens,
        d_gates,
        grad_up.astype(jnp.bfloat16)[None],
        grad_down.astype(jnp.bfloat16)[None],
    )


def shards(tokens, routes, gates, upstream, w_up, w_down):
    dense = 2 * routes.shape[1] >= lax.axis_size("expert") and lax.axis_size("tok") == 2
    body = dense_shards if dense else routed_shards
    return body(tokens, routes, gates, upstream, w_up, w_down)


def solution(mesh):
    return jax.shard_map(
        shards,
        mesh=mesh,
        in_specs=(
            P(("expert", "tok"), None),
            P(("expert", "tok"), None),
            P(("expert", "tok"), None),
            P(("expert", "tok"), None),
            P("expert", None, "tok"),
            P("expert", "tok", None),
        ),
        out_specs=(
            P(("expert", "tok"), None),
            P(("expert", "tok"), None),
            P(("expert", "tok"), None),
            P("expert", None, "tok"),
            P("expert", "tok", None),
        ),
        check_vma=False,
    )
```

profile of v0, /device:TPU:10, one launch (start us, length us, event | category | flops | bytes accessed | tf_op | source)
XLA Modules:
  0.0 600.3 jit_solution(6524580034297987019)
XLA Ops:
  7.2 0.0 all-gather.3.cloned.1.call-start
  7.2 0.7 all-gather.3.cloned.1.call-update
  7.9 0.0 all-gather.5.cloned.1.call-start
  7.9 0.7 all-gather.5.cloned.1.call-update
  8.6 0.0 reduce-scatter.5.cloned.1.call-start
  8.7 0.1 collective-permute-start
  8.8 0.5 collective-permute-start.1
  9.3 6.2 %collective-permute-done = bf16[3584,512]{1,0:T(8,128)(2,1)} collective-permute-done((bf16[3584,512]{1,0:T(8,128)(2,1)}, bf16[3584,512]{1,0:T(8,128)(2,1)}, u32[]{:S(2)}, u32[]{:S(2)}) %collective-permute-start) | collective-permute-done | bytes 3670048 | tf_op jit(solution)/shard_map/ppermute | solution.py:117
  15.5 98.8 %all-gather.3.cloned.1.call-done = bf16[1024,3584]{1,0:T(8,128)(2,1)} async-done(((bf16[64,3584]{1,0:T(8,128)(2,1)}), bf16[1024,3584]{1,0:T(8,128)(2,1)}) %all-gather.3.cloned.1.call-update) | async-done | bytes 7340048 | tf_op jit(solution)/shard_map/all_gather | solution.py:123
  114.3 13.6 %fusion.4 = f32[1024,1024]{1,0:T(8,128)} fusion(bf16[1024,3584]{1,0:T(8,128)(2,1)} %all-gather.3.cloned.1.call-done, bf16[3584,512]{1,0:T(8,128)(2,1)} %collective-permute-done, bf16[3584,512]{1,0:T(8,128)(2,1)} %bitcast.60), kind=kOutput, calls=%fused_computation.14 | convolution fusion | flops 7530872832 | bytes 18874368 | tf_op jit(solution)/shard_map/dot_general | solution.py:125
  127.9 0.0 copy-start.2
  127.9 0.0 copy-start.3
  127.9 0.0 collective-permute-done.1
  127.9 90.8 %all-gather.5.cloned.1.call-done = bf16[1024,3584]{1,0:T(8,128)(2,1)} async-done(((bf16[64,3584]{1,0:T(8,128)(2,1)}), bf16[1024,3584]{1,0:T(8,128)(2,1)}) %all-gather.5.cloned.1.call-update) | async-done | bytes 7340048 | tf_op jit(solution)/shard_map/all_gather | solution.py:124
  218.7 15.0 %fusion.12 = (f32[1024]{0:T(1024)S(1)}, f32[1024,1024]{1,0:T(8,128)}) fusion(f32[1024,1024]{1,0:T(8,128)} %fusion.4, bf16[1024,3584]{1,0:T(8,128)(2,1)} %all-gather.5.cloned.1.call-done, bf16[512,3584]{1,0:T(8,128)(2,1)} %collective-permute-done.1, bf16[512,3584]{1,0:T(8,128)(2,1)} %bitcast.63), kind=kOutput, calls=%fused_computation.24 | convolution fusion | flops 7541357568 | bytes 23072768 | tf_op jit(solution)/shard_map/dot_general | solution.py:131
  233.7 0.1 all_to_all.16
  233.7 10.0 %all_to_all.21 = f32[16,1,64]{2,1,0:T(1,128)S(1)} all-to-all(f32[16,1,64]{2,1,0:T(1,128)S(1)} %bitcast.56), channel_id=1, replica_groups=mesh['expert'=16,'tok'=2] {'expert'}, dimensions={0} | all-to-all | bytes 8192 | tf_op jit(solution)/shard_map/all_to_all | solution.py:142
  243.8 0.0 copy-done.2
  243.8 0.0 copy-done.3
  243.8 0.6 select_reduce_fusion
  244.4 9.8 %all_to_all.22 = f32[16,1,64]{2,1,0:T(1,128)S(1)} all-to-all(f32[16,1,64]{2,1,0:T(1,128)S(1)} %bitcast.55), channel_id=1, replica_groups=mesh['expert'=16,'tok'=2] {'expert'}, dimensions={0} | all-to-all | bytes 8192 | tf_op jit(solution)/shard_map/all_to_all | solution.py:121
  254.2 0.5 broadcast.46
  254.7 0.7 reduce.3
  255.4 0.1 mul.75
  255.5 0.0 copy-start.4
  255.5 5.6 fusion.11
  261.1 0.0 copy-start
  261.1 1.3 copy-done
  262.4 0.0 copy-done.4
  262.4 12.0 %convolution_convert_fusion = bf16[1024,3584]{1,0:T(8,128)(2,1)} fusion(bf16[1024,1024]{0,1:T(8,128)(2,1)S(1)} %get-tuple-element.27, bf16[3584,512]{1,0:T(8,128)(2,1)} %collective-permute-done, bf16[3584,512]{1,0:T(8,128)(2,1)S(1)} %bitcast.61), kind=kOutput, calls=%fused_computation | convolution fusion | flops 7534542848 | bytes 16777216 | tf_op jit(solution)/shard_map/dot_general | solution.py:136
  274.4 0.0 reduce-scatter.5.cloned.1.call-update
  274.4 0.3 reduce-scatter.3.cloned.1.call-start
  274.6 13.0 %convolution_convert_fusion.1 = bf16[1024,3584]{1,0:T(8,128)(2,1)} fusion(bf16[1024,1024]{0,1:T(8,128)(2,1)S(1)} %get-tuple-element.28, bf16[512,3584]{1,0:T(8,128)(2,1)} %collective-permute-done.1, bf16[512,3584]{1,0:T(8,128)(2,1)} %bitcast.64), kind=kOutput, calls=%fused_computation.1 | convolution fusion | flops 7534542848 | bytes 16777216 | tf_op jit(solution)/shard_map/dot_general | solution.py:127
  287.7 0.0 reduce-scatter.3.cloned.1.call-update
  287.7 0.0 slice-start
  287.7 7.5 %fusion.1 = bf16[3584,512]{0,1:T(8,128)(2,1)S(1)} fusion(bf16[1024,3584]{1,0:T(8,128)(2,1)} %all-gather.3.cloned.1.call-done, bf16[1024,1024]{0,1:T(8,128)(2,1)} %copy-done), kind=kOutput, calls=%fused_computation.11 | convolution fusion | flops 3759931392 | bytes 12058624 | tf_op jit(solution)/shard_map/dot_general | solution.py:148
  295.3 0.0 copy-start.1
  295.3 0.0 slice-start.1
  295.3 0.1 collective-permute-start.2
  295.4 8.7 %convolution_convert_fusion.2 = bf16[512,3584]{1,0:T(8,128)(2,1)} fusion(bf16[1024,3584]{1,0:T(8,128)(2,1)} %all-gather.5.cloned.1.call-done, bf16[1024,1024]{0,1:T(8,128)(2,1)S(1)} %get-tuple-element.28), kind=kOutput, calls=%fused_computation.9 | convolution fusion | flops 3759931392 | bytes 12058624 | tf_op jit(solution)/shard_map/dot_general | solution.py:148
  304.0 0.3 collective-permute-start.3
  304.4 0.0 collective-permute-done.2
  304.4 0.0 slice-done
  304.4 0.0 copy-done.1
  304.4 0.0 slice-done.1
  304.4 5.4 fusion.2
  309.8 5.9 copy.25
  315.7 0.0 collective-permute-done.3
  315.7 9.1 %fusion.14 = bf16[1,512,3584]{2,1,0:T(8,128)(2,1)} fusion(bf16[512,3584]{1,0:T(8,128)(2,1)} %collective-permute-done.3, bf16[1024,3584]{1,0:T(8,128)(2,1)} %all-gather.5.cloned.1.call-done, bf16[1024,1024]{0,1:T(8,128)(2,1)S(1)} %get-tuple-element.28), kind=kOutput, calls=%fused_computation.28 | convolution fusion | flops 3763601408 | bytes 15728640 | tf_op jit(solution)/shard_map/dot_general | solution.py:148
  324.8 107.0 %reduce-scatter.5.cloned.1.call-done = bf16[64,3584]{1,0:T(8,128)(2,1)} async-done(((bf16[1024,3584]{1,0:T(8,128)(2,1)}), bf16[64,3584]{1,0:T(8,128)(2,1)}) %reduce-scatter.5.cloned.1.call-update) | async-done | bytes 458768 | tf_op jit(solution)/shard_map/reduce_scatter | solution.py:139
  431.8 161.9 %reduce-scatter.3.cloned.1.call-done = bf16[64,3584]{1,0:T(8,128)(2,1)} async-done(((bf16[1024,3584]{1,0:T(8,128)(2,1)}), bf16[64,3584]{1,0:T(8,128)(2,1)}) %reduce-scatter.3.cloned.1.call-update) | async-done | bytes 458768 | tf_op jit(solution)/shard_map/reduce_scatter | solution.py:128
  (1 shorter events, 0.0 us)
Async XLA Ops:
  7.2 107.2 %all-gather.3.cloned.1.call-start = ((), (), s32[]{:S(2)}) async-start(), calls=%async_computation.4 | async-start | bytes 7798784 | tf_op jit(solution)/shard_map/all_gather | solution.py:123
  7.9 210.8 %all-gather.5.cloned.1.call-start = ((), (), s32[]{:S(2)}) async-start(), calls=%async_computation.6 | async-start | bytes 7798784 | tf_op jit(solution)/shard_map/all_gather | solution.py:124
  8.6 423.2 %reduce-scatter.5.cloned.1.call-start = ((), (), s32[]{:S(2)}) async-start(), calls=%async_computation.7 | async-start | bytes 7798784 | tf_op jit(solution)/shard_map/reduce_scatter | solution.py:139
  8.7 6.8 %collective-permute-start = (bf16[3584,512]{1,0:T(8,128)(2,1)}, bf16[3584,512]{1,0:T(8,128)(2,1)}, u32[]{:S(2)}, u32[]{:S(2)}) collective-permute-start(bf16[3584,512]{1,0:T(8,128)(2,1)} %bitcast.59), channel_id=1, source_target_pairs={{0,1},{1,0},{2,3},{3,2},{4,5},{5,4},{6,7},{7,6},{8,9},{9,8},{10,11... | collective-permute-start | bytes 11010056 | tf_op jit(solution)/shard_map/ppermute | solution.py:117
  8.8 119.1 %collective-permute-start.1 = (bf16[512,3584]{1,0:T(8,128)(2,1)}, bf16[512,3584]{1,0:T(8,128)(2,1)}, u32[]{:S(2)}, u32[]{:S(2)}) collective-permute-start(bf16[512,3584]{1,0:T(8,128)(2,1)} %bitcast.62), channel_id=1, source_target_pairs={{0,1},{1,0},{2,3},{3,2},{4,5},{5,4},{6,7},{7,6},{8,9},{9,8},{10,11... | collective-permute-start | bytes 11010056 | tf_op jit(solution)/shard_map/ppermute | solution.py:118
  127.9 115.9 %copy-start.2 = (s32[64,8]{0,1:T(8,128)S(1)}, s32[64,8]{0,1:T(8,128)}, u32[]{:S(2)}) copy-start(s32[64,8]{0,1:T(8,128)} %param.7) | copy-start | bytes 6148
  127.9 115.9 %copy-start.3 = (f32[64,8]{0,1:T(8,128)S(1)}, f32[64,8]{0,1:T(8,128)}, u32[]{:S(2)}) copy-start(f32[64,8]{0,1:T(8,128)} %param.8) | copy-start | bytes 6148
  255.5 6.9 %copy-start.4 = (bf16[1,3584,512]{2,1,0:T(8,128)(2,1)S(1)}, bf16[1,3584,512]{2,1,0:T(8,128)(2,1)}, u32[]{:S(2)}) copy-start(bf16[1,3584,512]{2,1,0:T(8,128)(2,1)} %param.10) | copy-start | bytes 11010052
  261.1 1.3 copy-start
  274.4 319.4 %reduce-scatter.3.cloned.1.call-start = ((), (), s32[]{:S(2)}) async-start(), calls=%async_computation.5 | async-start | bytes 7798784 | tf_op jit(solution)/shard_map/reduce_scatter | solution.py:128
  287.7 16.6 %slice-start = ((s8[7340032]{0:T(1024)(128)(4,1)}), s8[4194304]{0:T(1024)(128)(4,1)S(1)}, s32[]{:S(2)}) async-start(s8[7340032]{0:T(1024)(128)(4,1)} %bitcast.57), calls=%async_computation.8 | async-start | bytes 8388608
  295.3 9.1 %copy-start.1 = (bf16[1024,1024]{0,1:T(8,128)(2,1)S(1)}, bf16[1024,1024]{0,1:T(8,128)(2,1)}, u32[]{:S(2)}) copy-start(bf16[1024,1024]{0,1:T(8,128)(2,1)} %copy-done) | copy-start | bytes 6291460
  295.3 9.1 %slice-start.1 = ((s8[7340032]{0:T(1024)(128)(4,1)}), s8[3145728]{0:T(1024)(128)(4,1)S(1)}, s32[]{:S(2)}) async-start(s8[7340032]{0:T(1024)(128)(4,1)} %bitcast.57), calls=%async_computation.9 | async-start | bytes 6291456
  295.3 9.1 %collective-permute-start.2 = (bf16[3584,512]{0,1:T(8,128)(2,1)S(1)}, bf16[3584,512]{0,1:T(8,128)(2,1)S(1)}, u32[]{:S(2)}, u32[]{:S(2)}) collective-permute-start(bf16[3584,512]{0,1:T(8,128)(2,1)S(1)} %fusion.1), channel_id=1, source_target_pairs={{0,1},{1,0},{2,3},{3,2},{4,5},{5,4},{6,7},{7,6},{8,9},{9,8},{10,11... | collective-permute-start | bytes 11010056 | tf_op jit(solution)/shard_map/ppermute | solution.py:157
  304.0 11.7 %collective-permute-start.3 = (bf16[512,3584]{1,0:T(8,128)(2,1)}, bf16[512,3584]{1,0:T(8,128)(2,1)}, u32[]{:S(2)}, u32[]{:S(2)}) collective-permute-start(bf16[512,3584]{1,0:T(8,128)(2,1)} %convolution_convert_fusion.2), channel_id=1, source_target_pairs={{0,1},{1,0},{2,3},{3,2},{4,5},{5,4},{6,7},{7,6},{8,9},{9,8},{10,11... | collective-permute-start | bytes 11010056 | tf_op jit(solution)/shard_map/ppermute | solution.py:156
Sparse Core Ops, SparseCore 0:
  10.7 103.6 all-gather.2
  117.0 101.6 all-gather.4
  274.5 157.2 reduce-scatter.4
  434.6 159.1 reduce-scatter.2
where the time goes:
time: 601 us; the launch traced here: 600 us
  waiting for transfers between devices  466 us (78%)
  matrix products  84.3 us (14%)
  blocking collectives  19.9 us (3%)
  between operations  13.9 us (2%)
  local copies, waits for them, and re-layouts  7.92 us (1%)
  other arithmetic  6.87 us (1%)
    reduce_scatter x1, waiting for transfers between devices, dense_shards(): lax.psum_scatter(mixed_part.astype(jnp.bfloat16), 'expert', scatter_dimen...  162 us
    reduce_scatter x1, waiting for transfers between devices, dense_shards(): lax.psum_scatter(dx_part.astype(jnp.bfloat16), 'expert', scatter_dimensio...  107 us
    all_gather x1, waiting for transfers between devices, dense_shards(): all_x = lax.all_gather(tokens, 'expert', axis=0, tiled=True)  98.8 us
    all_gather x1, waiting for transfers between devices, dense_shards(): all_u = lax.all_gather(upstream, 'expert', axis=0, tiled=True)  90.8 us
    dot_general x4, matrix products, outer(): lax.dot_general(rows, columns, (((0,), (0,)), ((), ())), preferred_elemen...  30.7 us
    dot_general x1, matrix products, dense_shards(): lax.dot_general(all_u, down_full, (((1,), (1,)), ((), ())), preferred_ele...  15 us
    dot_general x1, matrix products, dense_shards(): hidden = jnp.dot(all_x, up_full, preferred_element_type=jnp.float32)  13.6 us
    dot_general x1, matrix products, dense_shards(): mixed_part = jnp.dot(gated, down_full, preferred_element_type=jnp.float32)  13 us
  transfers between devices with their start and end apart: 8, of which 5 were waited for; matrix products, arithmetic and copies ran while one was open for 11% of the time, Pallas kernels for 0%

commit v1 on v0

--- a/solution.py
+++ b/solution.py
@@ -120,8 +120,11 @@
     gate_of = jnp.sum(jnp.where(named, gates[:, :, None], 0.0), axis=1)
     gate = lax.all_to_all(gate_of.T, "expert", split_axis=0, concat_axis=0, tiled=True)
     gate = gate.reshape(-1)[:, None]
-    all_x = lax.all_gather(tokens, "expert", axis=0, tiled=True)
-    all_u = lax.all_gather(upstream, "expert", axis=0, tiled=True)
+    all_x, all_u = jnp.split(
+        lax.all_gather(jnp.concatenate([tokens, upstream], axis=1), "expert", axis=0, tiled=True),
+        [tokens.shape[1]],
+        axis=1,
+    )
     hidden = jnp.dot(all_x, up_full, preferred_element_type=jnp.float32)
     gated = (gate * gelu_value(hidden)).astype(jnp.bfloat16)
     mixed_part = jnp.dot(gated, down_full, preferred_element_type=jnp.float32)

time: 601 us -> 580 us (0.965)
  waiting for transfers between devices: 466 us -> 448 us
  local copies, waits for them, and re-layouts: 7.92 us -> 0.69 us
    reduce_scatter x1, waiting for transfers between devices: 107 us -> 162 us  [dense_shards(): lax.psum_scatter(dx_part.astype(jnp.bfloat16), 'expert', scatter_dimensio...]
    reduce_scatter x1, waiting for transfers between devices: 162 us -> 113 us  [dense_shards(): lax.psum_scatter(mixed_part.astype(jnp.bfloat16), 'expert', scatter_dimen...]
    all_gather x2 -> x1, waiting for transfers between devices: 190 us -> 166 us  [dense_shards(): lax.all_gather(jnp.concatenate([tokens, upstream], axis=1), 'expert', axi...]
    unnamed x15 -> x18, local copies, waits for them, and re-layouts: 7.26 us -> 0.04 us
  transfers between devices with their start and end apart: 8 -> 7, of which waited for: 5 -> 4; matrix products, arithmetic and copies ran while one was open for 11% -> 10% of each run, Pallas kernels for 0% -> 0%
where the time goes in v1:
time: 580 us; the launch traced here: 579 us
  waiting for transfers between devices  448 us (77%)
  matrix products  85 us (15%)
  blocking collectives  20.9 us (4%)
  between operations  13.9 us (2%)
  other arithmetic  9.96 us (2%)
    all_gather x1, waiting for transfers between devices, dense_shards(): lax.all_gather(jnp.concatenate([tokens, upstream], axis=1), 'expert', axi...  166 us
    reduce_scatter x1, waiting for transfers between devices, dense_shards(): lax.psum_scatter(dx_part.astype(jnp.bfloat16), 'expert', scatter_dimensio...  162 us
    reduce_scatter x1, waiting for transfers between devices, dense_shards(): lax.psum_scatter(mixed_part.astype(jnp.bfloat16), 'expert', scatter_dimen...  113 us
    dot_general x4, matrix products, outer(): lax.dot_general(rows, columns, (((0,), (0,)), ((), ())), preferred_elemen...  30.9 us
    dot_general x1, matrix products, dense_shards(): lax.dot_general(all_u, down_full, (((1,), (1,)), ((), ())), preferred_ele...  17.1 us
    dot_general x1, matrix products, dense_shards(): lax.dot_general(d_hidden, up_full, (((1,), (1,)), ((), ())), preferred_el...  12.6 us
    dot_general x1, matrix products, dense_shards(): hidden = jnp.dot(all_x, up_full, preferred_element_type=jnp.float32)  12.2 us
    dot_general x1, matrix products, dense_shards(): mixed_part = jnp.dot(gated, down_full, preferred_element_type=jnp.float32)  12.1 us
  transfers between devices with their start and end apart: 7, of which 4 were waited for; matrix products, arithmetic and copies ran while one was open for 10% of the time, Pallas kernels for 0%

profile of v1, /device:TPU:10, one launch (start us, length us, event | category | flops | bytes accessed | tf_op | source)
XLA Modules:
  0.0 579.4 jit_solution(14672776238427808939)
XLA Ops:
  7.2 0.0 all-gather.2.cloned.1.call-start
  7.2 2.1 pad_maximum_fusion.6
  9.4 0.0 all-gather.2.cloned.1.call-update
  9.4 0.0 reduce-scatter.3.cloned.1.call-start
  9.4 0.1 collective-permute-start
  9.5 0.5 collective-permute-start.1
  10.0 6.2 %collective-permute-done = bf16[3584,512]{1,0:T(8,128)(2,1)} collective-permute-done((bf16[3584,512]{1,0:T(8,128)(2,1)}, bf16[3584,512]{1,0:T(8,128)(2,1)}, u32[]{:S(2)}, u32[]{:S(2)}) %collective-permute-start) | collective-permute-done | bytes 3670048 | tf_op jit(solution)/shard_map/ppermute | solution.py:117
  16.2 166.1 %all-gather.2.cloned.1.call-done = bf16[1024,7168]{1,0:T(8,128)(2,1)} async-done(((bf16[64,7168]{1,0:T(8,128)(2,1)}), bf16[1024,7168]{1,0:T(8,128)(2,1)}) %all-gather.2.cloned.1.call-update) | async-done | bytes 14680080 | tf_op jit(solution)/shard_map/all_gather | solution.py:124
  182.3 12.2 %fusion.10 = f32[1024,1024]{0,1:T(8,128)S(1)} fusion(bf16[1024,7168]{1,0:T(8,128)(2,1)} %all-gather.2.cloned.1.call-done, bf16[3584,512]{1,0:T(8,128)(2,1)} %collective-permute-done, bf16[3584,512]{1,0:T(8,128)(2,1)} %bitcast.26), kind=kOutput, calls=%fused_computation.18 | convolution fusion | flops 7530872832 | bytes 18874368 | tf_op jit(solution)/shard_map/dot_general | solution.py:128
  194.6 0.0 copy-start
  194.6 0.0 copy-start.2
  194.6 0.0 copy-start.3
  194.6 0.0 collective-permute-done.1
  194.6 17.1 %multiply_reduce_fusion = (f32[1024]{0:T(1024)S(1)}, f32[1024,1024]{0,1:T(8,128)}) fusion(f32[1024,1024]{0,1:T(8,128)S(1)} %fusion.10, bf16[512,3584]{1,0:T(8,128)(2,1)} %collective-permute-done.1, bf16[512,3584]{1,0:T(8,128)(2,1)} %bitcast.23, bf16[1024,7168]{1,0:T(8,128)(2,1)} %all-gather.2.cloned.1.call-done), kind=kOutput, calls=%fused_computation.29 | convolution fusion | flops 7541357568 | bytes 23072768 | tf_op jit(solution)/shard_map/dot_general | solution.py:134
  211.7 0.0 copy-done
  211.7 0.1 all_to_all.16
  211.8 11.1 %all_to_all.21 = f32[16,1,64]{2,1,0:T(1,128)S(1)} all-to-all(f32[16,1,64]{2,1,0:T(1,128)S(1)} %bitcast.19), channel_id=1, replica_groups=mesh['expert'=16,'tok'=2] {'expert'}, dimensions={0} | all-to-all | bytes 8192 | tf_op jit(solution)/shard_map/all_to_all | solution.py:145
  222.9 0.0 copy-done.2
  222.9 0.0 copy-done.3
  222.9 0.6 select_reduce_fusion
  223.5 9.8 %all_to_all.22 = f32[16,1,64]{2,1,0:T(1,128)S(1)} all-to-all(f32[16,1,64]{2,1,0:T(1,128)S(1)} %bitcast.18), channel_id=1, replica_groups=mesh['expert'=16,'tok'=2] {'expert'}, dimensions={0} | all-to-all | bytes 8192 | tf_op jit(solution)/shard_map/all_to_all | solution.py:121
  233.4 0.5 broadcast.46
  233.9 0.7 reduce.3
  234.5 0.1 mul.75
  234.6 0.0 copy-start.4
  234.6 6.5 %fusion.26 = (bf16[1024,1024]{0,1:T(8,128)(2,1)}, bf16[1024,1024]{0,1:T(8,128)(2,1)S(1)}) fusion(f32[1024,1024]{0,1:T(8,128)} %copy-done, f32[1024,1024]{0,1:T(8,128)} %get-tuple-element.10, f32[1024]{0:T(1024)S(1)} %mul.75), kind=kLoop, calls=%fused_computation.28 | loop fusion | flops 24117248 | bytes 12587008 | tf_op jit(solution)/shard_map/convert_element_type | solution.py:138
  241.1 0.0 copy-done.4
  241.1 12.1 %convolution_convert_fusion.1 = bf16[1024,3584]{1,0:T(8,128)(2,1)} fusion(bf16[1024,1024]{0,1:T(8,128)(2,1)S(1)} %get-tuple-element.8, bf16[512,3584]{1,0:T(8,128)(2,1)} %collective-permute-done.1, bf16[512,3584]{1,0:T(8,128)(2,1)S(1)} %bitcast.24), kind=kOutput, calls=%fused_computation.1 | convolution fusion | flops 7534542848 | bytes 16777216 | tf_op jit(solution)/shard_map/dot_general | solution.py:130
  253.3 0.0 reduce-scatter.3.cloned.1.call-update
  253.3 0.0 reduce-scatter.5.cloned.1.call-start
  253.4 12.6 %convolution_convert_fusion = bf16[1024,3584]{1,0:T(8,128)(2,1)} fusion(bf16[1024,1024]{0,1:T(8,128)(2,1)} %get-tuple-element.7, bf16[3584,512]{1,0:T(8,128)(2,1)} %collective-permute-done, bf16[3584,512]{1,0:T(8,128)(2,1)} %bitcast.27), kind=kOutput, calls=%fused_computation | convolution fusion | flops 7534542848 | bytes 16777216 | tf_op jit(solution)/shard_map/dot_general | solution.py:139
  266.0 0.0 reduce-scatter.5.cloned.1.call-update
  266.0 0.0 slice-start
  266.0 0.0 slice-start.1
  266.0 9.4 %convolution_convert_fusion.3 = bf16[3584,512]{1,0:T(8,128)(2,1)} fusion(bf16[1024,7168]{1,0:T(8,128)(2,1)} %all-gather.2.cloned.1.call-done, bf16[1024,1024]{0,1:T(8,128)(2,1)} %get-tuple-element.7), kind=kOutput, calls=%fused_computation.9 | convolution fusion | flops 3759931392 | bytes 12058624 | tf_op jit(solution)/shard_map/dot_general | solution.py:151
  275.4 0.0 copy-start.1
  275.4 0.0 slice-start.2
  275.4 0.0 slice-start.3
  275.4 0.0 collective-permute-start.2
  275.4 8.6 %convolution_convert_fusion.2 = bf16[512,3584]{1,0:T(8,128)(2,1)} fusion(bf16[1024,7168]{1,0:T(8,128)(2,1)} %all-gather.2.cloned.1.call-done, bf16[1024,1024]{0,1:T(8,128)(2,1)S(1)} %get-tuple-element.8), kind=kOutput, calls=%fused_computation.8 | convolution fusion | flops 3759931392 | bytes 12058624 | tf_op jit(solution)/shard_map/dot_general | solution.py:151
  284.1 0.3 collective-permute-start.3
  284.4 0.0 collective-permute-done.2
  284.4 0.0 slice-done
  284.4 0.0 slice-done.1
  284.4 0.0 copy-done.1
  284.4 0.0 slice-done.2
  284.4 0.0 slice-done.3
  284.5 7.4 %fusion.14 = bf16[1,3584,512]{2,1,0:T(8,128)(2,1)} fusion(bf16[3584,512]{1,0:T(8,128)(2,1)} %collective-permute-done.2, bf16[1024,7168]{1,0:T(8,128)(2,1)S(1)} %bitcast.21, bf16[1024,1024]{0,1:T(8,128)(2,1)S(1)} %copy-done.1), kind=kOutput, calls=%fused_computation.20 | convolution fusion | flops 3763601408 | bytes 15728640 | tf_op jit(solution)/shard_map/dot_general | solution.py:151
  291.9 0.0 collective-permute-done.3
  291.9 5.5 fusion.17
  297.4 113.4 %reduce-scatter.3.cloned.1.call-done = bf16[64,3584]{1,0:T(8,128)(2,1)} async-done(((bf16[1024,3584]{1,0:T(8,128)(2,1)}), bf16[64,3584]{1,0:T(8,128)(2,1)}) %reduce-scatter.3.cloned.1.call-update) | async-done | bytes 458768 | tf_op jit(solution)/shard_map/reduce_scatter | solution.py:131
  410.8 162.0 %reduce-scatter.5.cloned.1.call-done = bf16[64,3584]{1,0:T(8,128)(2,1)} async-done(((bf16[1024,3584]{1,0:T(8,128)(2,1)}), bf16[64,3584]{1,0:T(8,128)(2,1)}) %reduce-scatter.5.cloned.1.call-update) | async-done | bytes 458768 | tf_op jit(solution)/shard_map/reduce_scatter | solution.py:142
  (1 shorter events, 0.0 us)
Async XLA Ops:
  7.2 175.2 %all-gather.2.cloned.1.call-start = ((), (), s32[]{:S(2)}) async-start(), calls=%async_computation.4 | async-start | bytes 15597568 | tf_op jit(solution)/shard_map/all_gather | solution.py:124
  9.4 401.4 %reduce-scatter.3.cloned.1.call-start = ((), (), s32[]{:S(2)}) async-start(), calls=%async_computation.5 | async-start | bytes 7798784 | tf_op jit(solution)/shard_map/reduce_scatter | solution.py:131
  9.4 6.8 %collective-permute-start = (bf16[3584,512]{1,0:T(8,128)(2,1)}, bf16[3584,512]{1,0:T(8,128)(2,1)}, u32[]{:S(2)}, u32[]{:S(2)}) collective-permute-start(bf16[3584,512]{1,0:T(8,128)(2,1)} %bitcast.25), channel_id=1, source_target_pairs={{0,1},{1,0},{2,3},{3,2},{4,5},{5,4},{6,7},{7,6},{8,9},{9,8},{10,11... | collective-permute-start | bytes 11010056 | tf_op jit(solution)/shard_map/ppermute | solution.py:117
  9.5 185.1 %collective-permute-start.1 = (bf16[512,3584]{1,0:T(8,128)(2,1)}, bf16[512,3584]{1,0:T(8,128)(2,1)}, u32[]{:S(2)}, u32[]{:S(2)}) collective-permute-start(bf16[512,3584]{1,0:T(8,128)(2,1)} %bitcast.22), channel_id=1, source_target_pairs={{0,1},{1,0},{2,3},{3,2},{4,5},{5,4},{6,7},{7,6},{8,9},{9,8},{10,11... | collective-permute-start | bytes 11010056 | tf_op jit(solution)/shard_map/ppermute | solution.py:118
  194.6 17.1 %copy-start = (f32[1024,1024]{0,1:T(8,128)}, f32[1024,1024]{0,1:T(8,128)S(1)}, u32[]{:S(2)}) copy-start(f32[1024,1024]{0,1:T(8,128)S(1)} %fusion.10) | copy-start | bytes 12582916
  194.6 28.3 %copy-start.2 = (s32[64,8]{0,1:T(8,128)S(1)}, s32[64,8]{0,1:T(8,128)}, u32[]{:S(2)}) copy-start(s32[64,8]{0,1:T(8,128)} %param.7) | copy-start | bytes 6148
  194.6 28.3 %copy-start.3 = (f32[64,8]{0,1:T(8,128)S(1)}, f32[64,8]{0,1:T(8,128)}, u32[]{:S(2)}) copy-start(f32[64,8]{0,1:T(8,128)} %param.8) | copy-start | bytes 6148
  234.6 6.5 %copy-start.4 = (bf16[1,512,3584]{2,1,0:T(8,128)(2,1)S(1)}, bf16[1,512,3584]{2,1,0:T(8,128)(2,1)}, u32[]{:S(2)}) copy-start(bf16[1,512,3584]{2,1,0:T(8,128)(2,1)} %param.11) | copy-start | bytes 11010052
  253.3 319.5 %reduce-scatter.5.cloned.1.call-start = ((), (), s32[]{:S(2)}) async-start(), calls=%async_computation.6 | async-start | bytes 7798784 | tf_op jit(solution)/shard_map/reduce_scatter | solution.py:142
  266.0 18.4 %slice-start = ((s8[14680064]{0:T(1024)(128)(4,1)}), s8[4194304]{0:T(1024)(128)(4,1)S(1)}, s32[]{:S(2)}) async-start(s8[14680064]{0:T(1024)(128)(4,1)} %bitcast.20), calls=%async_computation.7 | async-start | bytes 8388608
  266.0 18.4 %slice-start.1 = ((s8[14680064]{0:T(1024)(128)(4,1)}), s8[4194304]{0:T(1024)(128)(4,1)S(1)}, s32[]{:S(2)}) async-start(s8[14680064]{0:T(1024)(128)(4,1)} %bitcast.20), calls=%async_computation.8 | async-start | bytes 8388608
  275.4 9.0 %copy-start.1 = (bf16[1024,1024]{0,1:T(8,128)(2,1)S(1)}, bf16[1024,1024]{0,1:T(8,128)(2,1)}, u32[]{:S(2)}) copy-start(bf16[1024,1024]{0,1:T(8,128)(2,1)} %get-tuple-element.7) | copy-start | bytes 6291460
  275.4 9.0 %slice-start.2 = ((s8[14680064]{0:T(1024)(128)(4,1)}), s8[4194304]{0:T(1024)(128)(4,1)S(1)}, s32[]{:S(2)}) async-start(s8[14680064]{0:T(1024)(128)(4,1)} %bitcast.20), calls=%async_computation.9 | async-start | bytes 8388608
  275.4 9.0 %slice-start.3 = ((s8[14680064]{0:T(1024)(128)(4,1)}), s8[2097152]{0:T(1024)(128)(4,1)S(1)}, s32[]{:S(2)}) async-start(s8[14680064]{0:T(1024)(128)(4,1)} %bitcast.20), calls=%async_computation.10 | async-start | bytes 4194304
  275.4 9.0 %collective-permute-start.2 = (bf16[3584,512]{1,0:T(8,128)(2,1)}, bf16[3584,512]{1,0:T(8,128)(2,1)}, u32[]{:S(2)}, u32[]{:S(2)}) collective-permute-start(bf16[3584,512]{1,0:T(8,128)(2,1)} %convolution_convert_fusion.3), channel_id=1, source_target_pairs={{0,1},{1,0},{2,3},{3,2},{4,5},{5,4},{6,7},{7,6},{8,9},{9,8},{10,11... | collective-permute-start | bytes 11010056 | tf_op jit(solution)/shard_map/ppermute | solution.py:160
  284.1 7.8 %collective-permute-start.3 = (bf16[512,3584]{1,0:T(8,128)(2,1)}, bf16[512,3584]{1,0:T(8,128)(2,1)S(1)}, u32[]{:S(2)}, u32[]{:S(2)}) collective-permute-start(bf16[512,3584]{1,0:T(8,128)(2,1)} %convolution_convert_fusion.2), channel_id=1, source_target_pairs={{0,1},{1,0},{2,3},{3,2},{4,5},{5,4},{6,7},{7,6},{8,9},{9,8},{10,11... | collective-permute-start | bytes 11010056 | tf_op jit(solution)/shard_map/ppermute | solution.py:159
Sparse Core Ops, SparseCore 0:
  11.3 170.9 all-gather.1
  253.4 157.3 reduce-scatter.2
  413.7 159.1 reduce-scatter.4
